TPU v7x, 32 devices: a whole 2x2x4 slice. The times are simulated.
32 devices in a mesh: groups: 2 (over y), ctx: 4 (over z), head: 2 (over x), sub: 2 (over core).
Axes of the slice: x: 2, y: 2, z: 4, core: 2. Of those that a mesh axis runs over, the one named last changes fastest.
Arguments:
- hidden_in: bfloat16 [1024, 5120], P(('groups', 'ctx'), 'sub'), parts along dimension 0, may hold values from -6 to 6
- w_qkv: bfloat16 [5120, 8, 896], P('sub', 'head', 'ctx'), may hold values from -0.078125 to 0.078125
- qkv_bias: bfloat16 [8, 896], P('head'), may hold values from -3 to 3
- w_out: bfloat16 [8, 640, 5120], P('head', 'ctx'), may hold values from -0.078125 to 0.078125
- prev_keys: bfloat16 [1024, 8, 128], P(('groups', 'ctx', 'sub'), 'head'), parts along dimension 0, may hold values from -60 to 60
- prev_values: bfloat16 [1024, 8, 128], P(('groups', 'ctx', 'sub'), 'head'), parts along dimension 0, may hold values from -6 to 6
- shard_blocks: int32 [8], P('groups'), parts along dimension 0, may hold values from 0 to 3, each once
Outputs:
- attn_out: bfloat16 [1024, 5120], P(('groups', 'ctx', 'sub'), 'head'), parts along dimension 0
There are 2 independent parts, one for each index of `groups`. A program takes and returns all parts, laid end to end along the dimension named above; an argument that names none is the same for every part. Nothing has to cross between parts.
Inputs may be any that keep to these rules, and one draw needn't show every extreme that they name: Index c of ctx holds the positions shard_blocks[c] * 128 to shard_blocks[c] * 128 + 127; every block occurs once.
All inputs are finite; a program needn't handle non-finite values.
Results may differ from a plain program's by a relative error of at most 0.015.
The roundings to bfloat16 on the way count: a program that leaves them out, or rounds other values in their place, can miss the bound.
Values may be sent and summed in bfloat16 or wider, within the bound.
No kernel may reach another device: no remote copies, remote signals or barrier semaphores. Data moves between devices by JAX's collectives and lax.ppermute only.
A program may use at most 64 MiB of HBM per device.

v0:
```python
import math
import jax
import jax.numpy as jnp
from jax import lax
from jax.sharding import PartitionSpec as P

G = 5
HD = 128
NPREV = 2
rope_base = 10000000.0
neg_big = -1e30


def rotate(vectors, positions):
    half_width = vectors.shape[-1] // 2
    frequency = rope_base ** (
        -(jnp.arange(half_width, dtype=jnp.float32) * 2.0) / vectors.shape[-1]
    )
    angles = positions.astype(jnp.float32)[:, None] * frequency[None, :]
    extra = (1,) * (vectors.ndim - 2)
    cosine = jnp.cos(angles).reshape((angles.shape[0],) + extra + (half_width,))
    sine_part = jnp.sin(angles).reshape((angles.shape[0],) + extra + (half_width,))
    first = vectors[..., :half_width]
    second = vectors[..., half_width:]
    return jnp.concatenate(
        [first * cosine - second * sine_part, second * cosine + first * sine_part], axis=-1
    )


def lookup(small_table, wanted):
    entries = jnp.arange(small_table.shape[0], dtype=jnp.int32)
    return jnp.sum(jnp.where(wanted[..., None] == entries, small_table, 0), axis=-1)


def local(hidden_in, w_qkv, qkv_bias, w_out, prev_keys, prev_values, shard_blocks):
    n_ctx = lax.axis_size("ctx")
    n_sub = lax.axis_size("sub")
    n_head = lax.axis_size("head")
    tok_ctx = hidden_in.shape[0]
    tok_dev = tok_ctx // n_sub
    span_len = tok_ctx * n_ctx // 2
    kv_dev = w_qkv.shape[1]
    me_ctx = lax.axis_index("ctx")
    me_sub = lax.axis_index("sub")
    partial_value = jnp.einsum(
        "td,dhn->thn",
        hidden_in,
        lax.all_gather(w_qkv, "ctx", axis=2, tiled=True),
        preferred_element_type=jnp.float32,
    )
    joined = lax.psum_scatter(partial_value, "sub", scatter_dimension=0, tiled=True)
    joined = (joined + qkv_bias.astype(jnp.float32)[None]).reshape(tok_dev, kv_dev, G + 2, HD)
    owner_block = lookup(shard_blocks, me_ctx)
    positions = owner_block * tok_ctx + me_sub * tok_dev + jnp.arange(tok_dev, dtype=jnp.int32)
    span_q = NPREV + positions // span_len
    local_q = positions % span_len
    queries = joined[:, :, :G]

    def arrange(rotated):
        return jnp.transpose(rotated.astype(jnp.bfloat16), (1, 0, 2, 3)).reshape(
            kv_dev, tok_dev * G, HD
        )

    q_intra = arrange(rotate(queries, local_q))
    q_succ = arrange(rotate(queries, local_q + span_len))
    q_inter = arrange(rotate(queries, jnp.full((tok_dev,), 2 * span_len - 1, jnp.int32)))
    k_cur = rotate(joined[:, :, G], local_q).astype(jnp.bfloat16)
    v_cur = joined[:, :, G + 1].astype(jnp.bfloat16)
    old_rows = (me_ctx * n_sub + me_sub) * tok_dev + jnp.arange(tok_dev, dtype=jnp.int32)
    k_prev = rotate(prev_keys.astype(jnp.float32), old_rows % span_len).astype(jnp.bfloat16)
    row_span = jnp.repeat(span_q, G)
    row_local = jnp.repeat(local_q, G)
    own_span = span_q[0]
    score_scale = HD ** (-0.5)
    row_count = tok_dev * G
    start_state = (
        jnp.full((kv_dev, row_count), neg_big, jnp.float32),
        jnp.zeros((kv_dev, row_count), jnp.float32),
        jnp.zeros((kv_dev, row_count, HD), jnp.float32),
    )

    def scores_of(query_set, key_block):
        return (
            jnp.einsum("hrd,khd->hrk", query_set, key_block, preferred_element_type=jnp.float32)
            * score_scale
        )

    def update(running, scores, allowed, value_block):
        running_max, weight_sum, weighted = running
        block_max = jnp.max(jnp.where(allowed, scores, neg_big), axis=2)
        new_max = jnp.maximum(running_max, block_max)
        weights = jnp.where(allowed, jnp.exp(scores - new_max[..., None]), 0.0)
        rescale = jnp.exp(running_max - new_max)
        weight_sum = weight_sum * rescale + jnp.sum(weights, axis=2)
        weighted = weighted * rescale[..., None] + jnp.einsum(
            "hrk,khd->hrd",
            weights.astype(jnp.bfloat16),
            value_block,
            preferred_element_type=jnp.float32,
        )
        return (new_max, weight_sum, weighted)

    def current_block(running, key_block, value_block, key_index):
        shard_index = key_index // tok_dev
        key_pos = (
            lookup(shard_blocks, shard_index // n_sub) * tok_ctx
            + shard_index % n_sub * tok_dev
            + key_index % tok_dev
        )
        key_span = NPREV + key_pos // span_len
        key_local = key_pos % span_len
        same_span = key_span[None, :] == row_span[:, None]
        before = key_span[None, :] == row_span[:, None] - 1
        allowed = same_span & (key_local[None, :] <= row_local[:, None]) | before
        query_set = jnp.where(key_span[0] == own_span, q_intra, q_succ)
        return update(running, scores_of(query_set, key_block), allowed[None], value_block)

    def earlier_block(running, key_block, value_block, key_index):
        block_span = key_index[0] // span_len
        query_set = jnp.where(block_span == own_span - 1, q_succ, q_inter)
        scores = scores_of(query_set, key_block)
        return update(running, scores, jnp.ones(scores.shape, jnp.bool_), value_block)

    cur_keys = lax.all_gather(k_cur, ("ctx", "sub"), axis=0, tiled=True)
    cur_values = lax.all_gather(v_cur, ("ctx", "sub"), axis=0, tiled=True)
    old_keys = lax.all_gather(k_prev, ("ctx", "sub"), axis=0, tiled=True)
    old_values = lax.all_gather(prev_values, ("ctx", "sub"), axis=0, tiled=True)
    piece_rows = cur_keys.shape[0]
    block_rows = math.gcd(piece_rows, tok_dev)

    def turn(turn_index, state_in):
        offset = turn_index * block_rows
        key_index = offset + jnp.arange(block_rows, dtype=jnp.int32)

        def take(values):
            return lax.dynamic_slice_in_dim(values, offset, block_rows, 0)

        state_in = current_block(state_in, take(cur_keys), take(cur_values), key_index)
        return earlier_block(state_in, take(old_keys), take(old_values), key_index)

    running_max, weight_sum, weighted = lax.fori_loop(
        0, piece_rows // block_rows, turn, start_state
    )
    head_out = (weighted / weight_sum[..., None]).astype(jnp.bfloat16)
    head_out = jnp.transpose(head_out.reshape(kv_dev, tok_dev, G, HD), (1, 0, 2, 3)).reshape(
        tok_dev, kv_dev, G * HD
    )
    group_cols = w_out.shape[2] // (n_head * n_sub)
    split_cols = w_out.reshape(kv_dev, w_out.shape[1], n_head, n_sub, group_cols)
    own_cols = lax.dynamic_index_in_dim(split_cols, me_sub, 3, keepdims=False).reshape(
        kv_dev, w_out.shape[1], n_head * group_cols
    )
    pair_heads = lax.all_gather(head_out, "sub", axis=0, tiled=True)
    summed = jnp.einsum(
        "thn,hnd->td",
        pair_heads,
        lax.all_gather(own_cols, "ctx", axis=1, tiled=True),
        preferred_element_type=jnp.float32,
    )
    shares = lax.psum_scatter(summed.astype(jnp.bfloat16), "head", scatter_dimension=1, tiled=True)
    return lax.all_to_all(shares, "sub", split_axis=0, concat_axis=1, tiled=True)


def solution(mesh):
    return jax.shard_map(
        local,
        mesh=mesh,
        in_specs=(
            P(("groups", "ctx"), "sub"),
            P("sub", "head", "ctx"),
            P("head", None),
            P("head", "ctx", None),
            P(("groups", "ctx", "sub"), "head", None),
            P(("groups", "ctx", "sub"), "head", None),
            P("groups"),
        ),
        out_specs=P(("groups", "ctx", "sub"), "head"),
        check_vma=False,
    )
```

profile of v0, /device:TPU:0, one launch (start us, length us, event | category | flops | bytes accessed | tf_op | source)
XLA Modules:
  0.0 695.2 jit_solution(7797207133418223826)
XLA Ops:
  6.5 0.7 all-gather.4.cloned.1.call-update
  7.3 317.9 %all-gather.4.cloned.1.call-done = bf16[2560,4,896]{0,2,1:T(8,128)(2,1)} async-done(((bf16[2560,4,224]{0,2,1:T(8,128)(2,1)}), bf16[2560,4,896]{0,2,1:T(8,128)(2,1)}) %all-gather.4.cloned.1.call-update) | async-done | bytes 18350096 | tf_op jit(solution)/shard_map/all_gather | solution.py:48
  325.2 13.3 %fusion.36 = f32[128,4,896]{2,0,1:T(8,128)} fusion(bf16[2560,4,896]{0,2,1:T(8,128)(2,1)} %all-gather.4.cloned.1.call-done, bf16[128,2560]{1,0:T(8,128)(2,1)S(1)} %copy-done), kind=kOutput, calls=%fused_computation.72 | convolution fusion | flops 2348810240 | bytes 20840448 | tf_op jit(solution)/shard_map/td,dhn->thn/dot_general | solution.py:45
  338.5 0.2 all-gather.6.cloned.1.call-start
  338.8 15.2 %reshape.509 = bf16[4,160,2,2,1280]{4,3,2,1,0:T(2,128)(2,1)} reshape(bf16[4,160,5120]{2,1,0:T(8,128)(2,1)} %param.12) | data formatting | bytes 13107200 | tf_op jit(solution)/shard_map/reshape | solution.py:149
  354.0 55.3 %dynamic-slice_reduce_fusion = bf16[4,160,2,1280]{3,2,1,0:T(2,128)(2,1)} fusion(bf16[4,160,2,2,1280]{4,3,2,1,0:T(2,128)(2,1)} %reshape.509, s32[]{:T(128)S(6)} %select_n.317), kind=kLoop, calls=%fused_computation.63 | loop fusion | bytes 6553604 | tf_op jit(solution)/shard_map/jit(dynamic_index_in_dim)/dynamic_slice | solution.py:150
  409.3 8.2 %reshape.510 = bf16[4,160,2560]{2,1,0:T(8,128)(2,1)} reshape(bf16[4,160,2,1280]{3,2,1,0:T(2,128)(2,1)} %dynamic-slice_reduce_fusion) | data formatting | bytes 6553600 | tf_op jit(solution)/shard_map/reshape | solution.py:150
  417.7 0.6 fusion.38
  419.1 0.4 multiply_cosine_fusion
  419.7 16.1 %all_gather.23 = bf16[512,4,128]{2,0,1:T(8,128)(2,1)S(1)} all-gather(bf16[64,4,128]{2,0,1:T(8,128)(2,1)S(1)} %pad_maximum_fusion.1), channel_id=1, replica_groups=mesh['groups'=2,'ctx'=4,'head'=2,'sub'=2] {'ctx','sub'}, dimensions={0}, use_global_device_ids=true | all-gather | bytes 589824 | tf_op jit(solution)/shard_map/all_gather | solution.py:126
  435.9 26.1 %all_gather.25 = bf16[512,4,128]{2,0,1:T(8,128)(2,1)} all-gather(bf16[64,4,128]{2,0,1:T(8,128)(2,1)S(1)} %copy.42), channel_id=1, replica_groups=mesh['groups'=2,'ctx'=4,'head'=2,'sub'=2] {'ctx','sub'}, dimensions={0}, use_global_device_ids=true | all-gather | bytes 589824 | tf_op jit(solution)/shard_map/all_gather | solution.py:127
  462.0 1.2 broadcast_add_fusion.1
  463.9 30.2 %all_gather.22 = bf16[512,4,128]{2,0,1:T(8,128)(2,1)} all-gather(bf16[64,4,128]{2,0,1:T(8,128)(2,1)S(1)} %pad_maximum_fusion), channel_id=1, replica_groups=mesh['groups'=2,'ctx'=4,'head'=2,'sub'=2] {'ctx','sub'}, dimensions={0}, use_global_device_ids=true | all-gather | bytes 589824 | tf_op jit(solution)/shard_map/all_gather | solution.py:124
  494.1 27.9 %all-gather = bf16[512,4,1,128]{3,2,0,1:T(2,128)(2,1)S(1)} all-gather(bf16[64,4,1,128]{3,2,0,1:T(2,128)(2,1)S(1)} %slice.97), channel_id=2, replica_groups=mesh['groups'=2,'ctx'=4,'head'=2,'sub'=2] {'ctx','sub'}, dimensions={0}, use_global_device_ids=true | all-gather | bytes 589824 | tf_op jit(solution)/shard_map/all_gather | solution.py:125
  522.0 1.1 subtract_convert_fusion
  523.2 0.4 maximum_bitcast_fusion.2
  523.5 0.4 copy.40
  524.0 0.4 maximum_bitcast_fusion.1
  524.4 0.4 copy.39
  524.9 0.4 maximum_bitcast_fusion
  525.2 0.4 copy.38
  525.7 34.2 %while.21 = (s32[]{:T(128)}, f32[4,320]{1,0:T(4,128)S(1)}, f32[4,320]{1,0:T(4,128)S(1)}, f32[4,320,128]{2,1,0:T(8,128)S(1)}, s32[4]{0:T(128)S(1)}, /*index=5*/s3...) while((s32[]{:T(128)}, f32[4,320]{1,0:T(4,128)S(1)}, ...), condition=%wide.region_8.9_spmd.clone, body=%wide.region_2.8_spmd.clone.sunk | while | flops 86380112 | bytes 6466017 | solution.py:141
  526.7 1.1 select_reduce_fusion.5
  527.8 0.3 fusion.64
  528.3 0.6 fusion.70
  528.8 1.2 convolution_add_fusion.3
  530.7 0.1 eq.213
  530.9 1.1 select_reduce_fusion.5
  532.0 0.3 fusion.64
  532.5 0.6 fusion.70
  533.1 1.2 convolution_add_fusion.3
  535.2 1.1 select_reduce_fusion.5
  536.3 0.3 fusion.64
  536.8 0.6 fusion.70
  537.4 1.2 convolution_add_fusion.3
  539.5 1.1 select_reduce_fusion.5
  540.6 0.3 fusion.64
  541.1 0.6 fusion.70
  541.7 1.2 convolution_add_fusion.3
  543.8 1.1 select_reduce_fusion.5
  544.9 0.3 fusion.64
  545.4 0.6 fusion.70
  545.9 1.2 convolution_add_fusion.3
  548.0 1.1 select_reduce_fusion.5
  549.2 0.3 fusion.64
  549.7 0.6 fusion.70
  550.2 1.2 convolution_add_fusion.3
  552.3 1.1 select_reduce_fusion.5
  553.4 0.3 fusion.64
  553.9 0.6 fusion.70
  554.5 1.2 convolution_add_fusion.3
  556.6 1.1 select_reduce_fusion.5
  557.7 0.3 fusion.64
  558.2 0.6 fusion.70
  558.8 1.2 convolution_add_fusion.3
  560.0 0.2 divide_convert_fusion
  560.2 0.3 copy.46
  560.6 0.4 reshape.508
  561.0 2.4 all_gather.26
  563.4 96.7 %all-gather.6.cloned.1.call-done = bf16[4,640,2560]{2,1,0:T(8,128)(2,1)} async-done(((bf16[4,160,2560]{2,1,0:T(8,128)(2,1)}), bf16[4,640,2560]{2,1,0:T(8,128)(2,1)}) %all-gather.6.cloned.1.call-update) | async-done | bytes 13107216 | tf_op jit(solution)/shard_map/all_gather | solution.py:157
  660.1 7.5 %fusion.35 = bf16[128,2560]{1,0:T(8,128)(2,1)} fusion(bf16[128,4,640]{2,0,1:T(8,128)(2,1)S(1)} %all_gather.26, bf16[4,640,2560]{2,1,0:T(8,128)(2,1)} %all-gather.6.cloned.1.call-done), kind=kOutput, calls=%fused_computation.65 | convolution fusion | flops 1678049280 | bytes 14417920 | tf_op jit(solution)/shard_map/thn,hnd->td/dot_general | solution.py:154
  667.6 15.3 %reduce-scatter.5.cloned.1.call-done = bf16[128,1280]{1,0:T(8,128)(2,1)} async-done(((bf16[128,2560]{1,0:T(8,128)(2,1)}), bf16[128,1280]{1,0:T(8,128)(2,1)}) %reduce-scatter.5.cloned.1.call-update) | async-done | bytes 327696 | tf_op jit(solution)/shard_map/reduce_scatter | solution.py:160
  682.9 5.0 all_to_all.19
  687.9 0.7 copy.52
  (161 shorter events, 8.4 us)
Async XLA Ops:
  6.5 318.6 %copy-start = (bf16[128,2560]{1,0:T(8,128)(2,1)S(1)}, bf16[128,2560]{1,0:T(8,128)(2,1)}, u32[]{:S(2)}) copy-start(bf16[128,2560]{1,0:T(8,128)(2,1)} %param.9) | copy-start | bytes 1966084
  6.5 318.6 %all-gather.4.cloned.1.call-start = ((), (), s32[]{:S(2)}) async-start(), calls=%async_computation.3 | async-start | bytes 22937600 | tf_op jit(solution)/shard_map/all_gather | solution.py:48
  7.3 454.7 %reduce-scatter.3.cloned.1.call-start = ((), (), s32[]{:S(2)}) async-start(), calls=%async_computation.4 | async-start | bytes 2752512 | tf_op jit(solution)/shard_map/reduce_scatter | solution.py:51
  338.5 321.5 %all-gather.6.cloned.1.call-start = ((), (), s32[]{:S(2)}) async-start(), calls=%async_computation.5 | async-start | bytes 16384000 | tf_op jit(solution)/shard_map/all_gather | solution.py:157
  409.3 8.3 %copy-start.5 = (s32[4]{0:T(128)S(1)}, s32[4]{0:T(128)}, u32[]{:S(2)}) copy-start(s32[4]{0:T(128)} %param.15) | copy-start | bytes 52
  409.3 9.7 %copy-start.4 = (bf16[4,896]{1,0:T(4,128)(2,1)S(1)}, bf16[4,896]{1,0:T(4,128)(2,1)}, u32[]{:S(2)}) copy-start(bf16[4,896]{1,0:T(4,128)(2,1)} %param.11) | copy-start | bytes 21508
  409.3 9.7 %copy-start.3 = (bf16[64,4,128]{2,1,0:T(4,128)(2,1)S(1)}, bf16[64,4,128]{2,1,0:T(4,128)(2,1)}, u32[]{:S(2)}) copy-start(bf16[64,4,128]{2,1,0:T(4,128)(2,1)} %param.14) | copy-start | bytes 196612
  409.3 9.7 %copy-start.2 = (bf16[64,4,128]{2,1,0:T(4,128)(2,1)S(1)}, bf16[64,4,128]{2,1,0:T(4,128)(2,1)}, u32[]{:S(2)}) copy-start(bf16[64,4,128]{2,1,0:T(4,128)(2,1)} %param.13) | copy-start | bytes 196612
  417.6 265.3 %reduce-scatter.5.cloned.1.call-start = ((), (), s32[]{:S(2)}) async-start(), calls=%async_computation.6 | async-start | bytes 983040 | tf_op jit(solution)/shard_map/reduce_scatter | solution.py:160
  561.0 127.7 %copy-start.1 = (bf16[128,2560]{1,0:T(8,128)(2,1)S(1)}, bf16[128,2560]{1,0:T(8,128)(2,1)}, u32[]{:S(2)}) copy-start(bf16[128,2560]{1,0:T(8,128)(2,1)} %param.9) | copy-start | bytes 1966084
Sparse Core Ops, SparseCore 0:
  8.9 316.2 all-gather.3
  338.6 7.8 reduce-scatter.2
  417.7 242.2 all-gather.5
  667.7 15.1 reduce-scatter.4
where the time goes:
time: 697 us; the launch traced here: 695 us
  waiting for transfers between devices  431 us (62%)
  blocking collectives  108 us (15%)
  local copies, waits for them, and re-layouts  85.7 us (12%)
  matrix products  45.5 us (7%)
  between operations  14.1 us (2%)
  other arithmetic  8.88 us (1%)
    all_gather x1, waiting for transfers between devices, local(): lax.all_gather(w_qkv, 'ctx', axis=2, tiled=True)  318 us
    all_gather x1, waiting for transfers between devices, local(): lax.all_gather(own_cols, 'ctx', axis=1, tiled=True)  96.7 us
    dynamic_slice x1, local copies, waits for them, and re-layouts, local(): lax.dynamic_index_in_dim(split_cols, me_sub, 3, keepdims=False)  55.3 us
    all_gather x1, blocking collectives, local(): cur_keys = lax.all_gather(k_cur, ('ctx', 'sub'), axis=0, tiled=True)  30.2 us
    all_gather x1, blocking collectives, local(): cur_values = lax.all_gather(v_cur, ('ctx', 'sub'), axis=0, tiled=True)  27.9 us
    all_gather x1, blocking collectives, local(): old_values = lax.all_gather(prev_values, ('ctx', 'sub'), axis=0, tiled=True)  26.1 us
    all_gather x1, blocking collectives, local(): old_keys = lax.all_gather(k_prev, ('ctx', 'sub'), axis=0, tiled=True)  16.1 us
    reduce_scatter x1, waiting for transfers between devices, local(): lax.psum_scatter(summed.astype(jnp.bfloat16), 'head', scatter_dimension=1...  15.3 us
  transfers between devices with their start and end apart: 4, of which 3 were waited for; matrix products, arithmetic and copies ran while one was open for 17% of the time, Pallas kernels for 0%

commit v1 on v0

--- a/solution.py
+++ b/solution.py
@@ -9,6 +9,24 @@
 NPREV = 2
 rope_base = 10000000.0
 neg_big = -1e30
+
+
+def on_each_block(array, axis, dim, apply, out_dim):
+    peers, mine, extent = (lax.axis_size(axis), lax.axis_index(axis), array.shape[dim])
+    right = [(i, (i + 1) % peers) for i in range(peers)]
+    held, result = (array, None)
+    for turn in range(peers):
+        owner = (mine - turn) % peers
+        coming = lax.ppermute(held, axis, right) if turn < peers - 1 else None
+        made = apply(held, owner * extent)
+        length = made.shape[out_dim]
+        if result is None:
+            result = jnp.zeros(
+                (*made.shape[:out_dim], peers * length, *made.shape[out_dim + 1 :]), made.dtype
+            )
+        result = lax.dynamic_update_slice_in_dim(result, made, owner * length, axis=out_dim)
+        held = coming
+    return result
 
 
 def rotate(vectors, positions):
@@ -42,11 +60,14 @@
     kv_dev = w_qkv.shape[1]
     me_ctx = lax.axis_index("ctx")
     me_sub = lax.axis_index("sub")
-    partial_value = jnp.einsum(
-        "td,dhn->thn",
-        hidden_in,
-        lax.all_gather(w_qkv, "ctx", axis=2, tiled=True),
-        preferred_element_type=jnp.float32,
+    partial_value = on_each_block(
+        w_qkv,
+        "ctx",
+        2,
+        lambda part, start: jnp.einsum(
+            "td,dhn->thn", hidden_in, part, preferred_element_type=jnp.float32
+        ),
+        2,
     )
     joined = lax.psum_scatter(partial_value, "sub", scatter_dimension=0, tiled=True)
     joined = (joined + qkv_bias.astype(jnp.float32)[None]).reshape(tok_dev, kv_dev, G + 2, HD)

time: 697 us -> 684 us (0.981)
  waiting for transfers between devices: 431 us -> 399 us
  local copies, waits for them, and re-layouts: 85.7 us -> 101 us
    all_gather x1 -> x0, waiting for transfers between devices: 318 us -> none  [local(): lax.all_gather(w_qkv, 'ctx', axis=2, tiled=True)]
    ppermute x0 -> x3, waiting for transfers between devices: none -> 285 us  [on_each_block(): coming = lax.ppermute(held, axis, right) if turn < peers - 1 else None]
    unnamed x0 -> x4, matrix products: none -> 14.5 us
    dot_general x1 -> x0, matrix products: 13.3 us -> none  [local(): jnp.einsum('td,dhn->thn', hidden_in, lax.all_gather(w_qkv, 'ctx', axis=2,...]
    dynamic_update_slice x0 -> x4, local copies, waits for them, and re-layouts: none -> 11.1 us  [on_each_block(): lax.dynamic_update_slice_in_dim(result, made, owner * length, axis=out_dim)]
  transfers between devices with their start and end apart: 4 -> 6, of which waited for: 3 -> 5; matrix products, arithmetic and copies ran while one was open for 17% -> 20% of each run, Pallas kernels for 0% -> 0%
where the time goes in v1:
time: 684 us; the launch traced here: 683 us
  waiting for transfers between devices  399 us (58%)
  blocking collectives  106 us (15%)
  local copies, waits for them, and re-layouts  101 us (15%)
  matrix products  46.7 us (7%)
  between operations  15.9 us (2%)
  other arithmetic  8.94 us (1%)
    ppermute x3, waiting for transfers between devices, on_each_block(): coming = lax.ppermute(held, axis, right) if turn < peers - 1 else None  285 us
    all_gather x1, waiting for transfers between devices, local(): lax.all_gather(own_cols, 'ctx', axis=1, tiled=True)  97.8 us
    dynamic_slice x1, local copies, waits for them, and re-layouts, local(): lax.dynamic_index_in_dim(split_cols, me_sub, 3, keepdims=False)  55.3 us
    all_gather x1, blocking collectives, local(): cur_keys = lax.all_gather(k_cur, ('ctx', 'sub'), axis=0, tiled=True)  29.1 us
    all_gather x1, blocking collectives, local(): cur_values = lax.all_gather(v_cur, ('ctx', 'sub'), axis=0, tiled=True)  28.5 us
    all_gather x1, blocking collectives, local(): old_values = lax.all_gather(prev_values, ('ctx', 'sub'), axis=0, tiled=True)  24 us
    all_gather x1, blocking collectives, local(): old_keys = lax.all_gather(k_prev, ('ctx', 'sub'), axis=0, tiled=True)  17 us
    reduce_scatter x1, waiting for transfers between devices, local(): lax.psum_scatter(summed.astype(jnp.bfloat16), 'head', scatter_dimension=1...  15.6 us
  transfers between devices with their start and end apart: 6, of which 5 were waited for; matrix products, arithmetic and copies ran while one was open for 20% of the time, Pallas kernels for 0%

profile of v1, /device:TPU:0, one launch (start us, length us, event | category | flops | bytes accessed | tf_op | source)
XLA Modules:
  0.0 682.9 jit_solution(6855947114044422506)
XLA Ops:
  7.4 3.1 collective-permute-start
  10.4 101.2 %collective-permute-done = bf16[2560,4,224]{0,2,1:T(8,128)(2,1)S(1)} collective-permute-done((bf16[2560,4,224]{0,2,1:T(8,128)(2,1)}, bf16[2560,4,224]{0,2,1:T(8,128)(2,1)S(1)}, u32[]{:S(2)}, u32[]{:S(2)}) %collective-permute-start) | collective-permute-done | bytes 4587552 | tf_op jit(solution)/shard_map/ppermute | solution.py:20
  111.7 2.1 copy-done.3
  113.7 102.1 %collective-permute-done.1 = bf16[2560,4,224]{0,2,1:T(8,128)(2,1)} collective-permute-done((bf16[2560,4,224]{0,2,1:T(8,128)(2,1)S(1)}, bf16[2560,4,224]{0,2,1:T(8,128)(2,1)}, u32[]{:S(2)}, u32[]{:S(2)}) %collective-permute-start.1) | collective-permute-done | bytes 4587552 | tf_op jit(solution)/shard_map/ppermute | solution.py:20
  215.8 3.6 fusion.44
  219.8 2.4 dynamic_update_slice.12
  222.2 3.6 fusion.45
  226.0 2.3 dynamic_update_slice.13
  228.3 3.6 fusion.46
  232.2 3.2 dynamic_update_slice.14
  235.4 81.8 %collective-permute-done.2 = bf16[2560,4,224]{0,2,1:T(8,128)(2,1)} collective-permute-done((bf16[2560,4,224]{0,2,1:T(8,128)(2,1)}, bf16[2560,4,224]{0,2,1:T(8,128)(2,1)}, u32[]{:S(2)}, u32[]{:S(2)}) %collective-permute-start.2) | collective-permute-done | bytes 4587552 | tf_op jit(solution)/shard_map/ppermute | solution.py:20
  317.2 3.6 fusion.47
  321.1 3.2 dynamic_update_slice.15
  324.3 1.2 copy-done.2
  325.8 15.2 %reshape.509 = bf16[4,160,2,2,1280]{4,3,2,1,0:T(2,128)(2,1)} reshape(bf16[4,160,5120]{2,1,0:T(8,128)(2,1)} %param.12) | data formatting | bytes 13107200 | tf_op jit(solution)/shard_map/reshape | solution.py:170
  341.0 55.3 %dynamic-slice_reduce_fusion = bf16[4,160,2,1280]{3,2,1,0:T(2,128)(2,1)} fusion(bf16[4,160,2,2,1280]{4,3,2,1,0:T(2,128)(2,1)} %reshape.509, s32[]{:T(128)S(6)} %select_n.355), kind=kLoop, calls=%fused_computation.63 | loop fusion | bytes 6553604 | tf_op jit(solution)/shard_map/jit(dynamic_index_in_dim)/dynamic_slice | solution.py:171
  396.3 8.2 %reshape.510 = bf16[4,160,2560]{2,1,0:T(8,128)(2,1)} reshape(bf16[4,160,2,1280]{3,2,1,0:T(2,128)(2,1)} %dynamic-slice_reduce_fusion) | data formatting | bytes 6553600 | tf_op jit(solution)/shard_map/reshape | solution.py:171
  404.7 0.7 fusion.36
  406.2 0.4 multiply_cosine_fusion
  406.9 17.0 %all_gather.19 = bf16[512,4,128]{2,0,1:T(8,128)(2,1)S(1)} all-gather(bf16[64,4,128]{2,0,1:T(8,128)(2,1)S(1)} %pad_maximum_fusion.1), channel_id=1, replica_groups=mesh['groups'=2,'ctx'=4,'head'=2,'sub'=2] {'ctx','sub'}, dimensions={0}, use_global_device_ids=true | all-gather | bytes 589824 | tf_op jit(solution)/shard_map/all_gather | solution.py:147
  423.8 24.0 %all_gather.21 = bf16[512,4,128]{2,0,1:T(8,128)(2,1)} all-gather(bf16[64,4,128]{2,0,1:T(8,128)(2,1)S(1)} %copy.52), channel_id=1, replica_groups=mesh['groups'=2,'ctx'=4,'head'=2,'sub'=2] {'ctx','sub'}, dimensions={0}, use_global_device_ids=true | all-gather | bytes 589824 | tf_op jit(solution)/shard_map/all_gather | solution.py:148
  447.9 1.2 broadcast_add_fusion.1
  449.8 29.1 %all_gather.18 = bf16[512,4,128]{2,0,1:T(8,128)(2,1)} all-gather(bf16[64,4,128]{2,0,1:T(8,128)(2,1)S(1)} %pad_maximum_fusion), channel_id=1, replica_groups=mesh['groups'=2,'ctx'=4,'head'=2,'sub'=2] {'ctx','sub'}, dimensions={0}, use_global_device_ids=true | all-gather | bytes 589824 | tf_op jit(solution)/shard_map/all_gather | solution.py:145
  478.9 28.5 %all-gather = bf16[512,4,1,128]{3,2,0,1:T(2,128)(2,1)S(1)} all-gather(bf16[64,4,1,128]{3,2,0,1:T(2,128)(2,1)S(1)} %slice.97), channel_id=2, replica_groups=mesh['groups'=2,'ctx'=4,'head'=2,'sub'=2] {'ctx','sub'}, dimensions={0}, use_global_device_ids=true | all-gather | bytes 589824 | tf_op jit(solution)/shard_map/all_gather | solution.py:146
  507.5 1.1 subtract_convert_fusion
  508.6 0.4 maximum_bitcast_fusion.2
  509.0 0.4 copy.50
  509.5 0.4 maximum_bitcast_fusion.1
  509.8 0.4 copy.49
  510.3 0.4 maximum_bitcast_fusion
  510.7 0.4 copy.48
  511.2 34.2 %while.21 = (s32[]{:T(128)}, f32[4,320]{1,0:T(4,128)S(1)}, f32[4,320]{1,0:T(4,128)S(1)}, f32[4,320,128]{2,1,0:T(8,128)S(1)}, s32[4]{0:T(128)S(1)}, /*index=5*/s3...) while((s32[]{:T(128)}, f32[4,320]{1,0:T(4,128)S(1)}, ...), condition=%wide.region_8.9_spmd.clone, body=%wide.region_2.8_spmd.clone.sunk | while | flops 86380112 | bytes 6466017 | solution.py:162
  512.1 1.1 select_reduce_fusion.5
  513.2 0.3 fusion.73
  513.7 0.6 fusion.79
  514.3 1.2 convolution_add_fusion.3
  516.4 1.1 select_reduce_fusion.5
  518.0 0.6 fusion.79
  518.5 1.2 convolution_add_fusion.3
  520.7 1.1 select_reduce_fusion.5
  522.3 0.6 fusion.79
  522.8 1.2 convolution_add_fusion.3
  524.9 1.1 select_reduce_fusion.5
  526.5 0.6 fusion.79
  527.1 1.2 convolution_add_fusion.3
  529.2 1.1 select_reduce_fusion.5
  530.8 0.6 fusion.79
  531.4 1.2 convolution_add_fusion.3
  533.5 1.1 select_reduce_fusion.5
  535.1 0.6 fusion.79
  535.7 1.2 convolution_add_fusion.3
  537.8 1.1 select_reduce_fusion.5
  539.4 0.6 fusion.79
  539.9 1.2 convolution_add_fusion.3
  542.0 1.1 select_reduce_fusion.5
  543.6 0.6 fusion.79
  544.2 1.2 convolution_add_fusion.3
  546.0 0.4 reshape.508
  546.4 2.3 all_gather.22
  548.7 97.8 %all-gather.3.cloned.1.call-done = bf16[4,640,2560]{2,1,0:T(8,128)(2,1)} async-done(((bf16[4,160,2560]{2,1,0:T(8,128)(2,1)}), bf16[4,640,2560]{2,1,0:T(8,128)(2,1)}) %all-gather.3.cloned.1.call-update) | async-done | bytes 13107216 | tf_op jit(solution)/shard_map/all_gather | solution.py:178
  646.5 7.5 %fusion.35 = bf16[128,2560]{1,0:T(8,128)(2,1)} fusion(bf16[128,4,640]{2,0,1:T(8,128)(2,1)S(1)} %all_gather.22, bf16[4,640,2560]{2,1,0:T(8,128)(2,1)} %all-gather.3.cloned.1.call-done), kind=kOutput, calls=%fused_computation.65 | convolution fusion | flops 1678049280 | bytes 14417920 | tf_op jit(solution)/shard_map/thn,hnd->td/dot_general | solution.py:175
  654.0 15.6 %reduce-scatter.5.cloned.1.call-done = bf16[128,1280]{1,0:T(8,128)(2,1)} async-done(((bf16[128,2560]{1,0:T(8,128)(2,1)}), bf16[128,1280]{1,0:T(8,128)(2,1)}) %reduce-scatter.5.cloned.1.call-update) | async-done | bytes 327696 | tf_op jit(solution)/shard_map/reduce_scatter | solution.py:181
  669.6 5.0 all_to_all.19
  674.7 0.7 copy.62
  (180 shorter events, 11.9 us)
Async XLA Ops:
  7.4 208.4 %copy-start = (bf16[128,2560]{1,0:T(8,128)(2,1)S(1)}, bf16[128,2560]{1,0:T(8,128)(2,1)}, u32[]{:S(2)}) copy-start(bf16[128,2560]{1,0:T(8,128)(2,1)} %param.9) | copy-start | bytes 1966084
  7.4 440.5 %reduce-scatter.3.cloned.1.call-start = ((), (), s32[]{:S(2)}) async-start(), calls=%async_computation.3 | async-start | bytes 2752512 | tf_op jit(solution)/shard_map/reduce_scatter | solution.py:72
  7.4 104.3 %collective-permute-start = (bf16[2560,4,224]{0,2,1:T(8,128)(2,1)}, bf16[2560,4,224]{0,2,1:T(8,128)(2,1)S(1)}, u32[]{:S(2)}, u32[]{:S(2)}) collective-permute-start(bf16[2560,4,224]{0,2,1:T(8,128)(2,1)} %param.10), channel_id=1, source_target_pairs={{0,4},{4,8},{8,12},{12,0},{1,5},{5,9},{9,13},{13,1},{2,6},{6,10},{... | collective-permute-start | bytes 13762568 | tf_op jit(solution)/shard_map/ppermute | solution.py:20
  111.7 2.1 copy-start.3
  113.7 102.1 %collective-permute-start.1 = (bf16[2560,4,224]{0,2,1:T(8,128)(2,1)S(1)}, bf16[2560,4,224]{0,2,1:T(8,128)(2,1)}, u32[]{:S(2)}, u32[]{:S(2)}) collective-permute-start(bf16[2560,4,224]{0,2,1:T(8,128)(2,1)S(1)} %collective-permute-done), channel_id=1, source_target_pairs={{0,4},{4,8},{8,12},{12,0},{1,5},{5,9},{9,13},{13,1},{2,6},{6,10},{... | collective-permute-start | bytes 13762568 | tf_op jit(solution)/shard_map/ppermute | solution.py:20
  215.8 101.4 %collective-permute-start.2 = (bf16[2560,4,224]{0,2,1:T(8,128)(2,1)}, bf16[2560,4,224]{0,2,1:T(8,128)(2,1)}, u32[]{:S(2)}, u32[]{:S(2)}) collective-permute-start(bf16[2560,4,224]{0,2,1:T(8,128)(2,1)} %collective-permute-done.1), channel_id=1, source_target_pairs={{0,4},{4,8},{8,12},{12,0},{1,5},{5,9},{9,13},{13,1},{2,6},{6,10},{... | collective-permute-start | bytes 13762568 | tf_op jit(solution)/shard_map/ppermute | solution.py:20
  324.3 1.2 copy-start.2
  325.6 320.9 %all-gather.3.cloned.1.call-start = ((), (), s32[]{:S(2)}) async-start(), calls=%async_computation.4 | async-start | bytes 16384000 | tf_op jit(solution)/shard_map/all_gather | solution.py:178
  396.3 8.3 %copy-start.7 = (s32[4]{0:T(128)S(1)}, s32[4]{0:T(128)}, u32[]{:S(2)}) copy-start(s32[4]{0:T(128)} %param.15) | copy-start | bytes 52
  396.3 9.8 %copy-start.6 = (bf16[4,896]{1,0:T(4,128)(2,1)S(1)}, bf16[4,896]{1,0:T(4,128)(2,1)}, u32[]{:S(2)}) copy-start(bf16[4,896]{1,0:T(4,128)(2,1)} %param.11) | copy-start | bytes 21508
  396.3 9.8 %copy-start.5 = (bf16[64,4,128]{2,1,0:T(4,128)(2,1)S(1)}, bf16[64,4,128]{2,1,0:T(4,128)(2,1)}, u32[]{:S(2)}) copy-start(bf16[64,4,128]{2,1,0:T(4,128)(2,1)} %param.14) | copy-start | bytes 196612
  396.3 9.9 %copy-start.4 = (bf16[64,4,128]{2,1,0:T(4,128)(2,1)S(1)}, bf16[64,4,128]{2,1,0:T(4,128)(2,1)}, u32[]{:S(2)}) copy-start(bf16[64,4,128]{2,1,0:T(4,128)(2,1)} %param.13) | copy-start | bytes 196612
  404.6 265.1 %reduce-scatter.5.cloned.1.call-start = ((), (), s32[]{:S(2)}) async-start(), calls=%async_computation.5 | async-start | bytes 983040 | tf_op jit(solution)/shard_map/reduce_scatter | solution.py:181
  646.5 28.9 %copy-start.1 = (bf16[128,2560]{1,0:T(8,128)(2,1)S(1)}, bf16[128,2560]{1,0:T(8,128)(2,1)}, u32[]{:S(2)}) copy-start(bf16[128,2560]{1,0:T(8,128)(2,1)} %param.9) | copy-start | bytes 1966084
Sparse Core Ops, SparseCore 0:
  325.7 7.1 reduce-scatter.2
  654.2 15.4 reduce-scatter.4
Sparse Core Ops, SparseCore 1:
  404.7 241.8 all-gather.2
